TPU v7x, 32 devices: a whole 2x2x4 slice. The times are simulated.
32 devices in a mesh: gx: 4 (over y, x), gy: 8 (over z, core).
Axes of the slice: x: 2, y: 2, z: 4, core: 2. Of those that a mesh axis runs over, the one named last changes fastest.
Arguments:
- start_block: bfloat16 [64, 65536], P(None, ('gx', 'gy')), may hold values from -200 to 200
- tiles: bfloat16 [256, 10, 256, 256], P(('gx', 'gy')), may hold values from -0.125 to 0.125
- tile_cols: int32 [256, 10], P(('gx', 'gy')), may hold values from 0 to 15, as said below
- send_rows: int32 [32, 2], P(('gx', 'gy')), may hold values from 0 to 7, as said below
- shifts: float32 [4], replicated, may hold values from -1 to 1
Outputs:
- basis_q: float32 [256, 65536], P(None, ('gx', 'gy'))
Inputs may be any that keep to these rules, and one draw needn't show every extreme that they name: `tile_cols`: every tile-row's first tile is its own diagonal tile; values below 8 name the partition's own tile-rows, the others ghost slots in the extended order. `send_rows`: each partition's 2 entries are distinct own tile-rows.
All inputs are finite; a program needn't handle non-finite values.
Results may differ from a plain program's by a relative error of at most 0.009.
The roundings to bfloat16 on the way count: a program that leaves them out, or rounds other values in their place, can miss the bound.
Values may be sent and summed in bfloat16 or wider, within the bound.
A program may use at most 64 MiB of HBM per device.

v0:
```python
import jax
import jax.numpy as jnp
from jax import lax
from jax.sharding import PartitionSpec as P


def extended_2(block, sides, width):
    for axis, dim in sides:
        count = lax.axis_size(axis)
        forward = [(i, i + 1) for i in range(count - 1)]
        backward = [(target, source) for source, target in forward]
        low = lax.ppermute(
            lax.slice_in_dim(block, block.shape[dim] - width, None, axis=dim), axis, forward
        )
        high = lax.ppermute(lax.slice_in_dim(block, 0, width, axis=dim), axis, backward)
        block = jnp.concatenate([low, block, high], axis=dim)
    return block


def apply_local(current, tiles, flat_cols, send_list):
    width = current.shape[0]
    tile_rows, slots, tile, _ = tiles.shape
    own = current.reshape(width, tile_rows, tile)
    outgoing = jnp.take(own, send_list, axis=1)
    framed = extended_2(outgoing[None, None], (("gx", 0), ("gy", 1)), 1)
    extended = jnp.concatenate(
        [own, framed[0, 1], framed[2, 1], framed[1, 0], framed[1, 2]], axis=1
    )
    picked = jnp.take(extended, flat_cols, axis=1).reshape(width, tile_rows, slots, tile)
    image = jnp.einsum("ctkb,tkab->cta", picked, tiles, preferred_element_type=jnp.float32)
    return image.reshape(width, tile_rows * tile)


def body(start_block, tiles, tile_cols, send_rows, shifts):
    flat_cols = tile_cols.reshape(-1)
    send_list = send_rows[0]
    current = start_block
    blocks = []
    for step in range(shifts.shape[0]):
        image = apply_local(current, tiles, flat_cols, send_list)
        current = (image - shifts[step] * current.astype(jnp.float32)).astype(jnp.bfloat16)
        blocks.append(current)
    basis = jnp.concatenate(blocks, axis=0)
    total_rows = basis.shape[1] * lax.axis_size("gx") * lax.axis_size("gy")
    local_gram = (
        lax.dot_general(basis, basis, (((1,), (1,)), ((), ())), preferred_element_type=jnp.float32)
        / total_rows
    )
    lower = jnp.linalg.cholesky(lax.psum(local_gram, ("gx", "gy")))
    return lax.linalg.triangular_solve(lower, basis.astype(jnp.float32), left_side=True, lower=True)


def solution(mesh):
    in_specs = (
        P(None, ("gx", "gy")),
        P(("gx", "gy"), None, None, None),
        P(("gx", "gy"), None),
        P(("gx", "gy"), None),
        P(),
    )
    out_specs = P(None, ("gx", "gy"))
    return jax.shard_map(body, mesh=mesh, in_specs=in_specs, out_specs=out_specs, check_vma=False)
```

profile of v0, /device:TPU:0, one launch (start us, length us, event | category | flops | bytes accessed | tf_op | source)
XLA Modules:
  0.0 325.0 jit_solution(11236422951529813700)
XLA Ops:
  10.8 5.5 %collective-permute-start = (bf16[1,1,64,2,256]{4,2,3,1,0:T(8,128)(2,1)S(1)}, bf16[1,1,64,2,256]{4,2,3,1,0:T(8,128)(2,1)S(1)}, u32[]{:S(2)}, u32[]{:S(2)}) collective-permute-start(bf16[1,1,64,2,256]{4,2,3,1,0:T(8,128)(2,1)S(1)} %select_bitcast_fusion.3), channel_id=1, source_target_pairs={{0,8},{8,16},{16,24},{1,9},{9,17},{17,25},{2,10},{10,18},{18,26},{... | collective-permute-start | bytes 196616 | tf_op jit(solution)/shard_map/ppermute | solution.py:12
  18.0 1.5 fusion.28
  20.9 3.0 collective-permute-start.2
  26.1 7.3 %convolution_bitcast_fusion.3 = f32[8,8,8,256]{3,2,1,0:T(8,128)S(1)} fusion(bf16[64,8,10,256]{3,0,2,1:T(8,128)(2,1)S(1)} %bitcast.176, bf16[8,10,256,256]{3,2,1,0:T(8,128)(2,1)} %param.10), kind=kOutput, calls=%fused_computation.19 | convolution fusion | flops 671088640 | bytes 13631488 | tf_op jit(solution)/shard_map/ctkb,tkab->cta/dot_general | solution.py:30
  36.0 5.4 %collective-permute-start.4 = (bf16[1,1,64,2,256]{4,2,3,1,0:T(8,128)(2,1)S(1)}, bf16[1,1,64,2,256]{4,2,3,1,0:T(8,128)(2,1)S(1)}, u32[]{:S(2)}, u32[]{:S(2)}) collective-permute-start(bf16[1,1,64,2,256]{4,2,3,1,0:T(8,128)(2,1)S(1)} %select_bitcast_fusion.2), channel_id=1, source_target_pairs={{0,8},{8,16},{16,24},{1,9},{9,17},{17,25},{2,10},{10,18},{18,26},{... | collective-permute-start | bytes 196616 | tf_op jit(solution)/shard_map/ppermute | solution.py:12
  41.7 1.6 collective-permute-done.4
  44.7 4.4 %collective-permute-start.6 = (bf16[3,1,64,2,256]{4,2,3,1,0:T(8,128)(2,1)S(1)}, bf16[3,1,64,2,256]{4,2,3,1,0:T(8,128)(2,1)S(1)}, u32[]{:S(2)}, u32[]{:S(2)}) collective-permute-start(bf16[3,1,64,2,256]{4,2,3,1,0:T(8,128)(2,1)S(1)} %pad_maximum_fusion.2), channel_id=1, source_target_pairs={{0,1},{1,2},{2,3},{3,4},{4,5},{5,6},{6,7},{8,9},{9,10},{10,11},{11... | collective-permute-start | bytes 589832 | tf_op jit(solution)/shard_map/ppermute | solution.py:12
  51.2 7.3 %convolution_bitcast_fusion.2 = f32[8,8,8,256]{3,2,1,0:T(8,128)S(1)} fusion(bf16[64,8,10,256]{3,0,2,1:T(8,128)(2,1)S(1)} %bitcast.177, bf16[8,10,256,256]{3,2,1,0:T(8,128)(2,1)} %param.10), kind=kOutput, calls=%fused_computation.18 | convolution fusion | flops 671088640 | bytes 13631488 | tf_op jit(solution)/shard_map/ctkb,tkab->cta/dot_general | solution.py:30
  61.2 5.2 %collective-permute-start.8 = (bf16[1,1,64,2,256]{4,2,3,1,0:T(8,128)(2,1)S(1)}, bf16[1,1,64,2,256]{4,2,3,1,0:T(8,128)(2,1)S(1)}, u32[]{:S(2)}, u32[]{:S(2)}) collective-permute-start(bf16[1,1,64,2,256]{4,2,3,1,0:T(8,128)(2,1)S(1)} %select_bitcast_fusion.1), channel_id=1, source_target_pairs={{0,8},{8,16},{16,24},{1,9},{9,17},{17,25},{2,10},{10,18},{18,26},{... | collective-permute-start | bytes 196616 | tf_op jit(solution)/shard_map/ppermute | solution.py:12
  66.7 1.6 collective-permute-done.8
  68.3 1.3 collective-permute-start.11
  69.6 6.8 %collective-permute-start.10 = (bf16[3,1,64,2,256]{4,2,3,1,0:T(8,128)(2,1)S(1)}, bf16[3,1,64,2,256]{4,2,3,1,0:T(8,128)(2,1)S(1)}, u32[]{:S(2)}, u32[]{:S(2)}) collective-permute-start(bf16[3,1,64,2,256]{4,2,3,1,0:T(8,128)(2,1)S(1)} %pad_maximum_fusion.3), channel_id=1, source_target_pairs={{0,1},{1,2},{2,3},{3,4},{4,5},{5,6},{6,7},{8,9},{9,10},{10,11},{11... | collective-permute-start | bytes 589832 | tf_op jit(solution)/shard_map/ppermute | solution.py:12
  78.7 7.3 %convolution_bitcast_fusion.1 = f32[8,8,8,256]{3,2,1,0:T(8,128)S(1)} fusion(bf16[64,8,10,256]{3,0,2,1:T(8,128)(2,1)S(1)} %bitcast.178, bf16[8,10,256,256]{3,2,1,0:T(8,128)(2,1)} %param.10), kind=kOutput, calls=%fused_computation.17 | convolution fusion | flops 671088640 | bytes 13631488 | tf_op jit(solution)/shard_map/ctkb,tkab->cta/dot_general | solution.py:30
  88.7 5.8 %collective-permute-start.12 = (bf16[1,1,64,2,256]{4,2,3,1,0:T(8,128)(2,1)S(1)}, bf16[1,1,64,2,256]{4,2,3,1,0:T(8,128)(2,1)S(1)}, u32[]{:S(2)}, u32[]{:S(2)}) collective-permute-start(bf16[1,1,64,2,256]{4,2,3,1,0:T(8,128)(2,1)S(1)} %select_bitcast_fusion), channel_id=1, source_target_pairs={{0,8},{8,16},{16,24},{1,9},{9,17},{17,25},{2,10},{10,18},{18,26},{... | collective-permute-start | bytes 196616 | tf_op jit(solution)/shard_map/ppermute | solution.py:12
  94.8 1.6 collective-permute-done.12
  97.7 6.8 %collective-permute-start.14 = (bf16[3,1,64,2,256]{4,2,3,1,0:T(8,128)(2,1)S(1)}, bf16[3,1,64,2,256]{4,2,3,1,0:T(8,128)(2,1)S(1)}, u32[]{:S(2)}, u32[]{:S(2)}) collective-permute-start(bf16[3,1,64,2,256]{4,2,3,1,0:T(8,128)(2,1)S(1)} %pad_maximum_fusion.4), channel_id=1, source_target_pairs={{0,1},{1,2},{2,3},{3,4},{4,5},{5,6},{6,7},{8,9},{9,10},{10,11},{11... | collective-permute-start | bytes 589832 | tf_op jit(solution)/shard_map/ppermute | solution.py:12
  106.5 7.3 %convolution_bitcast_fusion = f32[8,8,8,256]{3,2,1,0:T(8,128)S(1)} fusion(bf16[64,8,10,256]{3,0,2,1:T(8,128)(2,1)S(1)} %bitcast.175, bf16[8,10,256,256]{3,2,1,0:T(8,128)(2,1)} %param.10), kind=kOutput, calls=%fused_computation.16 | convolution fusion | flops 671088640 | bytes 13631488 | tf_op jit(solution)/shard_map/ctkb,tkab->cta/dot_general | solution.py:30
  115.8 136.7 %all-reduce.3.cloned.1.call-done = f32[256,256]{0,1:T(8,128)} async-done(((f32[256,256]{0,1:T(8,128)}), f32[256,256]{0,1:T(8,128)}) %all-reduce.3.cloned.1.call-update) | async-done | bytes 262160 | tf_op jit(solution)/shard_map/psum | solution.py:49
  254.6 11.7 %cholesky.50 = f32[128,128]{1,0:T(8,128)S(1)} custom-call(f32[128,128]{1,0:T(8,128)S(1)} %cholesky.118), custom_call_target="Cholesky" | custom-call | tf_op jit(solution)/shard_map/jit(cholesky)/cholesky | solution.py:49
  266.4 9.8 %custom-call.14 = f32[1,128,128]{1,2,0:T(8,128)S(1)} custom-call(f32[1,128,128]{2,1,0:T(8,128)S(1)} %get-tuple-element.28), custom_call_target="InvertDiagBlocksLowerTriangular" | custom-call | tf_op jit(solution)/shard_map/jit(cholesky)/cholesky | solution.py:49
  276.7 11.9 %cholesky.105 = f32[128,128]{1,0:T(8,128)S(1)} custom-call(f32[128,128]{1,0:T(8,128)S(1)} %convolution_subtract_fusion.1), custom_call_target="Cholesky" | custom-call | tf_op jit(solution)/shard_map/jit(cholesky)/cholesky | solution.py:49
  290.5 3.8 %while.1 = (s32[]{:T(128)}, f32[256,256]{1,0:T(8,128)S(1)}, s32[2,2]{1,0:T(2,128)S(1)}, f32[2,128,128]{2,1,0:T(8,128)S(1)}, s32[]{:T(128)}) while((s32[]{:T(128)}, f32[256,256]{1,0:T(8,128)S(1)}, s32[2,2]{1,0:T(2,128)S(1)}, f32[2,128,128]{2,1,0:T(8,128)S(1)}, s32[]{:T(128)}) %tuple.28), condition=%wide.while_cond, body=%wide.while_body.sunk | while | flops 2 | bytes 131189 | solution.py:50
  294.3 19.7 %custom-call.15 = f32[2,128,128]{1,2,0:T(8,128)S(1)} custom-call(f32[2,128,128]{2,1,0:T(8,128)S(1)} %get-tuple-element.14), custom_call_target="InvertDiagBlocksLowerTriangular" | custom-call | tf_op jit(solution)/shard_map/triangular_solve | solution.py:50
  316.7 1.5 pad_maximum_fusion
  (116 shorter events, 38.9 us)
Async XLA Ops:
  6.5 246.0 %all-reduce.3.cloned.1.call-start = ((), (), s32[]{:S(2)}) async-start(), calls=%async_computation | async-start | bytes 524288 | tf_op jit(solution)/shard_map/psum | solution.py:49
  9.5 10.0 %collective-permute-start.1 = (bf16[1,1,64,2,256]{4,2,3,1,0:T(8,128)(2,1)S(1)}, bf16[1,1,64,2,256]{4,2,3,1,0:T(8,128)(2,1)S(1)}, u32[]{:S(2)}, u32[]{:S(2)}) collective-permute-start(bf16[1,1,64,2,256]{4,2,3,1,0:T(8,128)(2,1)S(1)} %select_bitcast_fusion.3), channel_id=1, source_target_pairs={{8,0},{16,8},{24,16},{9,1},{17,9},{25,17},{10,2},{18,10},{26,18},{... | collective-permute-start | bytes 196616 | tf_op jit(solution)/shard_map/ppermute | solution.py:15
  10.8 8.8 %collective-permute-start = (bf16[1,1,64,2,256]{4,2,3,1,0:T(8,128)(2,1)S(1)}, bf16[1,1,64,2,256]{4,2,3,1,0:T(8,128)(2,1)S(1)}, u32[]{:S(2)}, u32[]{:S(2)}) collective-permute-start(bf16[1,1,64,2,256]{4,2,3,1,0:T(8,128)(2,1)S(1)} %select_bitcast_fusion.3), channel_id=1, source_target_pairs={{0,8},{8,16},{16,24},{1,9},{9,17},{17,25},{2,10},{10,18},{18,26},{... | collective-permute-start | bytes 196616 | tf_op jit(solution)/shard_map/ppermute | solution.py:12
  19.6 5.4 %collective-permute-start.3 = (bf16[3,1,64,2,256]{4,2,3,1,0:T(8,128)(2,1)S(1)}, bf16[3,1,64,2,256]{4,2,3,1,0:T(8,128)(2,1)S(1)}, u32[]{:S(2)}, u32[]{:S(2)}) collective-permute-start(bf16[3,1,64,2,256]{4,2,3,1,0:T(8,128)(2,1)S(1)} %pad_maximum_fusion.1), channel_id=1, source_target_pairs={{1,0},{2,1},{3,2},{4,3},{5,4},{6,5},{7,6},{9,8},{10,9},{11,10},{12... | collective-permute-start | bytes 589832 | tf_op jit(solution)/shard_map/ppermute | solution.py:15
  20.9 4.1 %collective-permute-start.2 = (bf16[3,1,64,2,256]{4,2,3,1,0:T(8,128)(2,1)S(1)}, bf16[3,1,64,2,256]{4,2,3,1,0:T(8,128)(2,1)S(1)}, u32[]{:S(2)}, u32[]{:S(2)}) collective-permute-start(bf16[3,1,64,2,256]{4,2,3,1,0:T(8,128)(2,1)S(1)} %pad_maximum_fusion.1), channel_id=1, source_target_pairs={{0,1},{1,2},{2,3},{3,4},{4,5},{5,6},{6,7},{8,9},{9,10},{10,11},{11... | collective-permute-start | bytes 589832 | tf_op jit(solution)/shard_map/ppermute | solution.py:12
  26.1 7.3 %copy-start.5 = (bf16[64,2048]{1,0:T(8,128)(2,1)S(1)}, bf16[64,2048]{1,0:T(8,128)(2,1)}, u32[]{:S(2)}) copy-start(bf16[64,2048]{1,0:T(8,128)(2,1)} %param.9) | copy-start | bytes 786436
  34.7 7.0 %collective-permute-start.5 = (bf16[1,1,64,2,256]{4,2,3,1,0:T(8,128)(2,1)S(1)}, bf16[1,1,64,2,256]{4,2,3,1,0:T(8,128)(2,1)S(1)}, u32[]{:S(2)}, u32[]{:S(2)}) collective-permute-start(bf16[1,1,64,2,256]{4,2,3,1,0:T(8,128)(2,1)S(1)} %select_bitcast_fusion.2), channel_id=1, source_target_pairs={{8,0},{16,8},{24,16},{9,1},{17,9},{25,17},{10,2},{18,10},{26,18},{... | collective-permute-start | bytes 196616 | tf_op jit(solution)/shard_map/ppermute | solution.py:15
  36.0 7.3 %collective-permute-start.4 = (bf16[1,1,64,2,256]{4,2,3,1,0:T(8,128)(2,1)S(1)}, bf16[1,1,64,2,256]{4,2,3,1,0:T(8,128)(2,1)S(1)}, u32[]{:S(2)}, u32[]{:S(2)}) collective-permute-start(bf16[1,1,64,2,256]{4,2,3,1,0:T(8,128)(2,1)S(1)} %select_bitcast_fusion.2), channel_id=1, source_target_pairs={{0,8},{8,16},{16,24},{1,9},{9,17},{17,25},{2,10},{10,18},{18,26},{... | collective-permute-start | bytes 196616 | tf_op jit(solution)/shard_map/ppermute | solution.py:12
  43.4 6.8 %collective-permute-start.7 = (bf16[3,1,64,2,256]{4,2,3,1,0:T(8,128)(2,1)S(1)}, bf16[3,1,64,2,256]{4,2,3,1,0:T(8,128)(2,1)S(1)}, u32[]{:S(2)}, u32[]{:S(2)}) collective-permute-start(bf16[3,1,64,2,256]{4,2,3,1,0:T(8,128)(2,1)S(1)} %pad_maximum_fusion.2), channel_id=1, source_target_pairs={{1,0},{2,1},{3,2},{4,3},{5,4},{6,5},{7,6},{9,8},{10,9},{11,10},{12... | collective-permute-start | bytes 589832 | tf_op jit(solution)/shard_map/ppermute | solution.py:15
  44.7 5.5 %collective-permute-start.6 = (bf16[3,1,64,2,256]{4,2,3,1,0:T(8,128)(2,1)S(1)}, bf16[3,1,64,2,256]{4,2,3,1,0:T(8,128)(2,1)S(1)}, u32[]{:S(2)}, u32[]{:S(2)}) collective-permute-start(bf16[3,1,64,2,256]{4,2,3,1,0:T(8,128)(2,1)S(1)} %pad_maximum_fusion.2), channel_id=1, source_target_pairs={{0,1},{1,2},{2,3},{3,4},{4,5},{5,6},{6,7},{8,9},{9,10},{10,11},{11... | collective-permute-start | bytes 589832 | tf_op jit(solution)/shard_map/ppermute | solution.py:12
  59.3 18.3 %copy-start = (bf16[64,2048]{1,0:T(8,128)(2,1)}, bf16[64,2048]{1,0:T(8,128)(2,1)S(1)}, u32[]{:S(2)}) copy-start(bf16[64,2048]{1,0:T(8,128)(2,1)S(1)} %subtract_convert_fusion.2) | copy-start | bytes 786436
  59.9 6.8 %collective-permute-start.9 = (bf16[1,1,64,2,256]{4,2,3,1,0:T(8,128)(2,1)S(1)}, bf16[1,1,64,2,256]{4,2,3,1,0:T(8,128)(2,1)S(1)}, u32[]{:S(2)}, u32[]{:S(2)}) collective-permute-start(bf16[1,1,64,2,256]{4,2,3,1,0:T(8,128)(2,1)S(1)} %select_bitcast_fusion.1), channel_id=1, source_target_pairs={{8,0},{16,8},{24,16},{9,1},{17,9},{25,17},{10,2},{18,10},{26,18},{... | collective-permute-start | bytes 196616 | tf_op jit(solution)/shard_map/ppermute | solution.py:15
  61.2 7.1 %collective-permute-start.8 = (bf16[1,1,64,2,256]{4,2,3,1,0:T(8,128)(2,1)S(1)}, bf16[1,1,64,2,256]{4,2,3,1,0:T(8,128)(2,1)S(1)}, u32[]{:S(2)}, u32[]{:S(2)}) collective-permute-start(bf16[1,1,64,2,256]{4,2,3,1,0:T(8,128)(2,1)S(1)} %select_bitcast_fusion.1), channel_id=1, source_target_pairs={{0,8},{8,16},{16,24},{1,9},{9,17},{17,25},{2,10},{10,18},{18,26},{... | collective-permute-start | bytes 196616 | tf_op jit(solution)/shard_map/ppermute | solution.py:12
  68.3 9.2 %collective-permute-start.11 = (bf16[3,1,64,2,256]{4,2,3,1,0:T(8,128)(2,1)S(1)}, bf16[3,1,64,2,256]{4,2,3,1,0:T(8,128)(2,1)S(1)}, u32[]{:S(2)}, u32[]{:S(2)}) collective-permute-start(bf16[3,1,64,2,256]{4,2,3,1,0:T(8,128)(2,1)S(1)} %pad_maximum_fusion.3), channel_id=1, source_target_pairs={{1,0},{2,1},{3,2},{4,3},{5,4},{6,5},{7,6},{9,8},{10,9},{11,10},{12... | collective-permute-start | bytes 589832 | tf_op jit(solution)/shard_map/ppermute | solution.py:15
  69.6 7.9 %collective-permute-start.10 = (bf16[3,1,64,2,256]{4,2,3,1,0:T(8,128)(2,1)S(1)}, bf16[3,1,64,2,256]{4,2,3,1,0:T(8,128)(2,1)S(1)}, u32[]{:S(2)}, u32[]{:S(2)}) collective-permute-start(bf16[3,1,64,2,256]{4,2,3,1,0:T(8,128)(2,1)S(1)} %pad_maximum_fusion.3), channel_id=1, source_target_pairs={{0,1},{1,2},{2,3},{3,4},{4,5},{5,6},{6,7},{8,9},{9,10},{10,11},{11... | collective-permute-start | bytes 589832 | tf_op jit(solution)/shard_map/ppermute | solution.py:12
  78.6 7.3 %copy-start.1 = (bf16[64,2048]{1,0:T(8,128)(2,1)S(1)}, bf16[64,2048]{1,0:T(8,128)(2,1)}, u32[]{:S(2)}) copy-start(bf16[64,2048]{1,0:T(8,128)(2,1)} %copy-done) | copy-start | bytes 786436
  86.8 18.6 %copy-start.3 = (bf16[64,2048]{1,0:T(8,128)(2,1)}, bf16[64,2048]{1,0:T(8,128)(2,1)S(1)}, u32[]{:S(2)}) copy-start(bf16[64,2048]{1,0:T(8,128)(2,1)S(1)} %subtract_convert_fusion.1) | copy-start | bytes 786436
  87.4 7.4 %collective-permute-start.13 = (bf16[1,1,64,2,256]{4,2,3,1,0:T(8,128)(2,1)S(1)}, bf16[1,1,64,2,256]{4,2,3,1,0:T(8,128)(2,1)S(1)}, u32[]{:S(2)}, u32[]{:S(2)}) collective-permute-start(bf16[1,1,64,2,256]{4,2,3,1,0:T(8,128)(2,1)S(1)} %select_bitcast_fusion), channel_id=1, source_target_pairs={{8,0},{16,8},{24,16},{9,1},{17,9},{25,17},{10,2},{18,10},{26,18},{... | collective-permute-start | bytes 196616 | tf_op jit(solution)/shard_map/ppermute | solution.py:15
  88.7 7.7 %collective-permute-start.12 = (bf16[1,1,64,2,256]{4,2,3,1,0:T(8,128)(2,1)S(1)}, bf16[1,1,64,2,256]{4,2,3,1,0:T(8,128)(2,1)S(1)}, u32[]{:S(2)}, u32[]{:S(2)}) collective-permute-start(bf16[1,1,64,2,256]{4,2,3,1,0:T(8,128)(2,1)S(1)} %select_bitcast_fusion), channel_id=1, source_target_pairs={{0,8},{8,16},{16,24},{1,9},{9,17},{17,25},{2,10},{10,18},{18,26},{... | collective-permute-start | bytes 196616 | tf_op jit(solution)/shard_map/ppermute | solution.py:12
  96.4 8.9 %collective-permute-start.15 = (bf16[3,1,64,2,256]{4,2,3,1,0:T(8,128)(2,1)S(1)}, bf16[3,1,64,2,256]{4,2,3,1,0:T(8,128)(2,1)S(1)}, u32[]{:S(2)}, u32[]{:S(2)}) collective-permute-start(bf16[3,1,64,2,256]{4,2,3,1,0:T(8,128)(2,1)S(1)} %pad_maximum_fusion.4), channel_id=1, source_target_pairs={{1,0},{2,1},{3,2},{4,3},{5,4},{6,5},{7,6},{9,8},{10,9},{11,10},{12... | collective-permute-start | bytes 589832 | tf_op jit(solution)/shard_map/ppermute | solution.py:15
  97.7 7.6 %collective-permute-start.14 = (bf16[3,1,64,2,256]{4,2,3,1,0:T(8,128)(2,1)S(1)}, bf16[3,1,64,2,256]{4,2,3,1,0:T(8,128)(2,1)S(1)}, u32[]{:S(2)}, u32[]{:S(2)}) collective-permute-start(bf16[3,1,64,2,256]{4,2,3,1,0:T(8,128)(2,1)S(1)} %pad_maximum_fusion.4), channel_id=1, source_target_pairs={{0,1},{1,2},{2,3},{3,4},{4,5},{5,6},{6,7},{8,9},{9,10},{10,11},{11... | collective-permute-start | bytes 589832 | tf_op jit(solution)/shard_map/ppermute | solution.py:12
  106.5 7.4 %copy-start.4 = (bf16[64,2048]{1,0:T(8,128)(2,1)S(1)}, bf16[64,2048]{1,0:T(8,128)(2,1)}, u32[]{:S(2)}) copy-start(bf16[64,2048]{1,0:T(8,128)(2,1)} %copy-done.3) | copy-start | bytes 786436
  106.5 8.1 %copy-start.2 = (bf16[64,2048]{1,0:T(8,128)(2,1)S(1)}, bf16[64,2048]{1,0:T(8,128)(2,1)}, u32[]{:S(2)}) copy-start(bf16[64,2048]{1,0:T(8,128)(2,1)} %copy-done) | copy-start | bytes 786436
Sparse Core Ops, SparseCore 0:
  115.9 136.5 all-reduce.2
where the time goes:
time: 326 us; the launch traced here: 325 us
  waiting for transfers between devices  146 us (45%)
  other arithmetic  62.1 us (19%)
  starting transfers between devices  53.3 us (16%)
  matrix products  33.4 us (10%)
  between operations  15.3 us (5%)
  local copies, waits for them, and re-layouts  14.7 us (5%)
    psum x1, waiting for transfers between devices, body(): lower = jnp.linalg.cholesky(lax.psum(local_gram, ('gx', 'gy')))  137 us
    ppermute x8, starting transfers between devices, extended_2(): lax.ppermute(lax.slice_in_dim(block, block.shape[dim] - width, None, axis...  43 us
    another operation x6, other arithmetic, body(): lower = jnp.linalg.cholesky(lax.psum(local_gram, ('gx', 'gy')))  34.1 us
    dot_general x4, matrix products, apply_local(): jnp.einsum('ctkb,tkab->cta', picked, tiles, preferred_element_type=jnp.fl...  29.1 us
    another operation x4, other arithmetic, body(): lax.linalg.triangular_solve(lower, basis.astype(jnp.float32), left_side=T...  21.2 us
    ppermute x8, starting transfers between devices, extended_2(): lax.ppermute(lax.slice_in_dim(block, 0, width, axis=dim), axis, backward)  10.3 us
    ppermute x8, waiting for transfers between devices, extended_2(): lax.ppermute(lax.slice_in_dim(block, block.shape[dim] - width, None, axis...  8.61 us
  transfers between devices with their start and end apart: 17, of which 11 were waited for; matrix products, arithmetic and copies ran while one was open for 1% of the time, Pallas kernels for 0%

commit v1 on v0

--- a/solution.py
+++ b/solution.py
@@ -2,6 +2,11 @@
 import jax.numpy as jnp
 from jax import lax
 from jax.sharding import PartitionSpec as P
+
+
+def gather_and_add(shard, mesh_axis):
+    parts = lax.all_gather(shard, mesh_axis)
+    return jnp.sum(parts, axis=0)
 
 
 def extended_2(block, sides, width):
@@ -46,7 +51,7 @@
         lax.dot_general(basis, basis, (((1,), (1,)), ((), ())), preferred_element_type=jnp.float32)
         / total_rows
     )
-    lower = jnp.linalg.cholesky(lax.psum(local_gram, ("gx", "gy")))
+    lower = jnp.linalg.cholesky(gather_and_add(local_gram, ("gx", "gy")))
     return lax.linalg.triangular_solve(lower, basis.astype(jnp.float32), left_side=True, lower=True)
 
 

time: 326 us -> 278 us (0.85)
  waiting for transfers between devices: 146 us -> 109 us
  starting transfers between devices: 53.3 us -> 40.6 us
    psum x1 -> x0, waiting for transfers between devices: 137 us -> none  [body(): lower = jnp.linalg.cholesky(lax.psum(local_gram, ('gx', 'gy')))]
    all_gather x0 -> x1, waiting for transfers between devices: none -> 79.5 us  [gather_and_add(): parts = lax.all_gather(shard, mesh_axis)]
    ppermute x8, waiting for transfers between devices: 0.84 us -> 27.4 us  [extended_2(): lax.ppermute(lax.slice_in_dim(block, 0, width, axis=dim), axis, backward)]
    ppermute x8, starting transfers between devices: 43 us -> 30.1 us  [extended_2(): lax.ppermute(lax.slice_in_dim(block, block.shape[dim] - width, None, axis...]
    ppermute x8, waiting for transfers between devices: 8.61 us -> 1.69 us  [extended_2(): lax.ppermute(lax.slice_in_dim(block, block.shape[dim] - width, None, axis...]
    reduce_sum x0 -> x1, other arithmetic: none -> 3.93 us  [gather_and_add(): return jnp.sum(parts, axis=0)]
  transfers between devices with their start and end apart: 17 -> 17, of which waited for: 11 -> 12; matrix products, arithmetic and copies ran while one was open for 1% -> 1% of each run, Pallas kernels for 0% -> 0%
where the time goes in v1:
time: 278 us; the launch traced here: 277 us
  waiting for transfers between devices  109 us (39%)
  other arithmetic  65.1 us (23%)
  starting transfers between devices  40.6 us (15%)
  matrix products  33.4 us (12%)
  between operations  15.3 us (6%)
  local copies, waits for them, and re-layouts  13.8 us (5%)
    all_gather x1, waiting for transfers between devices, gather_and_add(): parts = lax.all_gather(shard, mesh_axis)  79.5 us
    another operation x6, other arithmetic, body(): lower = jnp.linalg.cholesky(gather_and_add(local_gram, ('gx', 'gy')))  34.2 us
    ppermute x8, starting transfers between devices, extended_2(): lax.ppermute(lax.slice_in_dim(block, block.shape[dim] - width, None, axis...  30.1 us
    dot_general x4, matrix products, apply_local(): jnp.einsum('ctkb,tkab->cta', picked, tiles, preferred_element_type=jnp.fl...  29.1 us
    ppermute x8, waiting for transfers between devices, extended_2(): lax.ppermute(lax.slice_in_dim(block, 0, width, axis=dim), axis, backward)  27.4 us
    another operation x4, other arithmetic, body(): lax.linalg.triangular_solve(lower, basis.astype(jnp.float32), left_side=T...  21.2 us
    ppermute x8, starting transfers between devices, extended_2(): lax.ppermute(lax.slice_in_dim(block, 0, width, axis=dim), axis, backward)  10.5 us
  transfers between devices with their start and end apart: 17, of which 12 were waited for; matrix products, arithmetic and copies ran while one was open for 1% of the time, Pallas kernels for 0%

profile of v1, /device:TPU:0, one launch (start us, length us, event | category | flops | bytes accessed | tf_op | source)
XLA Modules:
  0.0 276.8 jit_solution(18047211156065949003)
XLA Ops:
  9.5 4.9 %collective-permute-start = (bf16[1,1,64,2,256]{4,2,3,1,0:T(8,128)(2,1)S(1)}, bf16[1,1,64,2,256]{4,2,3,1,0:T(8,128)(2,1)S(1)}, u32[]{:S(2)}, u32[]{:S(2)}) collective-permute-start(bf16[1,1,64,2,256]{4,2,3,1,0:T(8,128)(2,1)S(1)} %select_bitcast_fusion.3), channel_id=1, source_target_pairs={{0,8},{8,16},{16,24},{1,9},{9,17},{17,25},{2,10},{10,18},{18,26},{... | collective-permute-start | bytes 196616 | tf_op jit(solution)/shard_map/ppermute | solution.py:17
  23.2 3.8 %collective-permute-done.3 = bf16[3,1,64,2,256]{4,2,3,1,0:T(8,128)(2,1)S(1)} collective-permute-done((bf16[3,1,64,2,256]{4,2,3,1,0:T(8,128)(2,1)S(1)}, bf16[3,1,64,2,256]{4,2,3,1,0:T(8,128)(2,1)S(1)}, u32[]{:S(2)}, u32[]{:S(2)}) %collective-permute-start.3) | collective-permute-done | bytes 196640 | tf_op jit(solution)/shard_map/ppermute | solution.py:20
  28.1 7.3 %convolution_bitcast_fusion.3 = f32[8,8,8,256]{3,2,1,0:T(8,128)S(1)} fusion(bf16[64,8,10,256]{3,0,2,1:T(8,128)(2,1)S(1)} %bitcast.177, bf16[8,10,256,256]{3,2,1,0:T(8,128)(2,1)} %param.10), kind=kOutput, calls=%fused_computation.19 | convolution fusion | flops 671088640 | bytes 13631488 | tf_op jit(solution)/shard_map/ctkb,tkab->cta/dot_general | solution.py:35
  36.7 4.3 %collective-permute-start.4 = (bf16[1,1,64,2,256]{4,2,3,1,0:T(8,128)(2,1)S(1)}, bf16[1,1,64,2,256]{4,2,3,1,0:T(8,128)(2,1)S(1)}, u32[]{:S(2)}, u32[]{:S(2)}) collective-permute-start(bf16[1,1,64,2,256]{4,2,3,1,0:T(8,128)(2,1)S(1)} %select_bitcast_fusion.2), channel_id=1, source_target_pairs={{0,8},{8,16},{16,24},{1,9},{9,17},{17,25},{2,10},{10,18},{18,26},{... | collective-permute-start | bytes 196616 | tf_op jit(solution)/shard_map/ppermute | solution.py:17
  42.9 4.7 %collective-permute-done.5 = bf16[1,1,64,2,256]{4,2,3,1,0:T(8,128)(2,1)S(1)} collective-permute-done((bf16[1,1,64,2,256]{4,2,3,1,0:T(8,128)(2,1)S(1)}, bf16[1,1,64,2,256]{4,2,3,1,0:T(8,128)(2,1)S(1)}, u32[]{:S(2)}, u32[]{:S(2)}) %collective-permute-start.5) | collective-permute-done | bytes 65568 | tf_op jit(solution)/shard_map/ppermute | solution.py:20
  47.6 4.2 %collective-permute-start.6 = (bf16[3,1,64,2,256]{4,2,3,1,0:T(8,128)(2,1)S(1)}, bf16[3,1,64,2,256]{4,2,3,1,0:T(8,128)(2,1)S(1)}, u32[]{:S(2)}, u32[]{:S(2)}) collective-permute-start(bf16[3,1,64,2,256]{4,2,3,1,0:T(8,128)(2,1)S(1)} %pad_maximum_fusion.2), channel_id=1, source_target_pairs={{0,1},{1,2},{2,3},{3,4},{4,5},{5,6},{6,7},{8,9},{9,10},{10,11},{11... | collective-permute-start | bytes 589832 | tf_op jit(solution)/shard_map/ppermute | solution.py:17
  53.2 2.8 %collective-permute-done.7 = bf16[3,1,64,2,256]{4,2,3,1,0:T(8,128)(2,1)S(1)} collective-permute-done((bf16[3,1,64,2,256]{4,2,3,1,0:T(8,128)(2,1)S(1)}, bf16[3,1,64,2,256]{4,2,3,1,0:T(8,128)(2,1)S(1)}, u32[]{:S(2)}, u32[]{:S(2)}) %collective-permute-start.7) | collective-permute-done | bytes 196640 | tf_op jit(solution)/shard_map/ppermute | solution.py:20
  57.1 7.2 %convolution_bitcast_fusion.2 = f32[8,8,8,256]{3,2,1,0:T(8,128)S(1)} fusion(bf16[64,8,10,256]{3,0,2,1:T(8,128)(2,1)S(1)} %bitcast.178, bf16[8,10,256,256]{3,2,1,0:T(8,128)(2,1)} %param.10), kind=kOutput, calls=%fused_computation.18 | convolution fusion | flops 671088640 | bytes 13631488 | tf_op jit(solution)/shard_map/ctkb,tkab->cta/dot_general | solution.py:35
  65.8 3.9 %collective-permute-start.8 = (bf16[1,1,64,2,256]{4,2,3,1,0:T(8,128)(2,1)S(1)}, bf16[1,1,64,2,256]{4,2,3,1,0:T(8,128)(2,1)S(1)}, u32[]{:S(2)}, u32[]{:S(2)}) collective-permute-start(bf16[1,1,64,2,256]{4,2,3,1,0:T(8,128)(2,1)S(1)} %select_bitcast_fusion.1), channel_id=1, source_target_pairs={{0,8},{8,16},{16,24},{1,9},{9,17},{17,25},{2,10},{10,18},{18,26},{... | collective-permute-start | bytes 196616 | tf_op jit(solution)/shard_map/ppermute | solution.py:17
  71.5 4.5 %collective-permute-done.9 = bf16[1,1,64,2,256]{4,2,3,1,0:T(8,128)(2,1)S(1)} collective-permute-done((bf16[1,1,64,2,256]{4,2,3,1,0:T(8,128)(2,1)S(1)}, bf16[1,1,64,2,256]{4,2,3,1,0:T(8,128)(2,1)S(1)}, u32[]{:S(2)}, u32[]{:S(2)}) %collective-permute-start.9) | collective-permute-done | bytes 65568 | tf_op jit(solution)/shard_map/ppermute | solution.py:20
  76.1 4.4 %collective-permute-start.10 = (bf16[3,1,64,2,256]{4,2,3,1,0:T(8,128)(2,1)S(1)}, bf16[3,1,64,2,256]{4,2,3,1,0:T(8,128)(2,1)S(1)}, u32[]{:S(2)}, u32[]{:S(2)}) collective-permute-start(bf16[3,1,64,2,256]{4,2,3,1,0:T(8,128)(2,1)S(1)} %pad_maximum_fusion.3), channel_id=1, source_target_pairs={{0,1},{1,2},{2,3},{3,4},{4,5},{5,6},{6,7},{8,9},{9,10},{10,11},{11... | collective-permute-start | bytes 589832 | tf_op jit(solution)/shard_map/ppermute | solution.py:17
  81.8 2.8 %collective-permute-done.11 = bf16[3,1,64,2,256]{4,2,3,1,0:T(8,128)(2,1)S(1)} collective-permute-done((bf16[3,1,64,2,256]{4,2,3,1,0:T(8,128)(2,1)S(1)}, bf16[3,1,64,2,256]{4,2,3,1,0:T(8,128)(2,1)S(1)}, u32[]{:S(2)}, u32[]{:S(2)}) %collective-permute-start.11) | collective-permute-done | bytes 196640 | tf_op jit(solution)/shard_map/ppermute | solution.py:20
  85.8 7.3 %convolution_bitcast_fusion.1 = f32[8,8,8,256]{3,2,1,0:T(8,128)S(1)} fusion(bf16[64,8,10,256]{3,0,2,1:T(8,128)(2,1)S(1)} %bitcast.179, bf16[8,10,256,256]{3,2,1,0:T(8,128)(2,1)} %param.10), kind=kOutput, calls=%fused_computation.17 | convolution fusion | flops 671088640 | bytes 13631488 | tf_op jit(solution)/shard_map/ctkb,tkab->cta/dot_general | solution.py:35
  94.6 2.7 collective-permute-start.12
  99.2 4.5 %collective-permute-done.13 = bf16[1,1,64,2,256]{4,2,3,1,0:T(8,128)(2,1)S(1)} collective-permute-done((bf16[1,1,64,2,256]{4,2,3,1,0:T(8,128)(2,1)S(1)}, bf16[1,1,64,2,256]{4,2,3,1,0:T(8,128)(2,1)S(1)}, u32[]{:S(2)}, u32[]{:S(2)}) %collective-permute-start.13) | collective-permute-done | bytes 65568 | tf_op jit(solution)/shard_map/ppermute | solution.py:20
  103.7 4.4 %collective-permute-start.14 = (bf16[3,1,64,2,256]{4,2,3,1,0:T(8,128)(2,1)S(1)}, bf16[3,1,64,2,256]{4,2,3,1,0:T(8,128)(2,1)S(1)}, u32[]{:S(2)}, u32[]{:S(2)}) collective-permute-start(bf16[3,1,64,2,256]{4,2,3,1,0:T(8,128)(2,1)S(1)} %pad_maximum_fusion.4), channel_id=1, source_target_pairs={{0,1},{1,2},{2,3},{3,4},{4,5},{5,6},{6,7},{8,9},{9,10},{10,11},{11... | collective-permute-start | bytes 589832 | tf_op jit(solution)/shard_map/ppermute | solution.py:17
  113.4 7.3 %convolution_bitcast_fusion = f32[8,8,8,256]{3,2,1,0:T(8,128)S(1)} fusion(bf16[64,8,10,256]{3,0,2,1:T(8,128)(2,1)S(1)} %bitcast.176, bf16[8,10,256,256]{3,2,1,0:T(8,128)(2,1)} %param.10), kind=kOutput, calls=%fused_computation.16 | convolution fusion | flops 671088640 | bytes 13631488 | tf_op jit(solution)/shard_map/ctkb,tkab->cta/dot_general | solution.py:35
  122.7 79.5 %all-gather.3.cloned.1.call-done = f32[8192,256]{1,0:T(8,128)} async-done(((f32[256,256]{1,0:T(8,128)}), f32[8192,256]{1,0:T(8,128)}) %all-gather.3.cloned.1.call-update) | async-done | bytes 8388624 | tf_op jit(solution)/shard_map/all_gather | solution.py:8
  202.2 3.9 %reduce_sum.9 = f32[256,256]{1,0:T(8,128)S(1)} reduce(f32[32,256,256]{2,1,0:T(8,128)} %bitcast.180, f32[]{:T(128)} %constant.95.clone.1), dimensions={0}, to_apply=%region_0.3 | reduce | flops 2031616 | bytes 8650756 | tf_op jit(solution)/shard_map/reduce_sum | solution.py:9
  206.3 11.7 %cholesky.50 = f32[128,128]{1,0:T(8,128)S(1)} custom-call(f32[128,128]{1,0:T(8,128)S(1)} %cholesky.118), custom_call_target="Cholesky" | custom-call | tf_op jit(solution)/shard_map/jit(cholesky)/cholesky | solution.py:54
  218.1 9.8 %custom-call.14 = f32[1,128,128]{1,2,0:T(8,128)S(1)} custom-call(f32[1,128,128]{2,1,0:T(8,128)S(1)} %get-tuple-element.28), custom_call_target="InvertDiagBlocksLowerTriangular" | custom-call | tf_op jit(solution)/shard_map/jit(cholesky)/cholesky | solution.py:54
  228.4 11.9 %cholesky.105 = f32[128,128]{1,0:T(8,128)S(1)} custom-call(f32[128,128]{1,0:T(8,128)S(1)} %convolution_subtract_fusion.1), custom_call_target="Cholesky" | custom-call | tf_op jit(solution)/shard_map/jit(cholesky)/cholesky | solution.py:54
  242.3 3.8 %while.1 = (s32[]{:T(128)}, f32[256,256]{1,0:T(8,128)S(1)}, s32[2,2]{1,0:T(2,128)S(1)}, f32[2,128,128]{2,1,0:T(8,128)S(1)}, s32[]{:T(128)}) while((s32[]{:T(128)}, f32[256,256]{1,0:T(8,128)S(1)}, s32[2,2]{1,0:T(2,128)S(1)}, f32[2,128,128]{2,1,0:T(8,128)S(1)}, s32[]{:T(128)}) %tuple.28), condition=%wide.while_cond, body=%wide.while_body.sunk | while | flops 2 | bytes 131181 | solution.py:55
  246.1 19.7 %custom-call.15 = f32[2,128,128]{1,2,0:T(8,128)S(1)} custom-call(f32[2,128,128]{2,1,0:T(8,128)S(1)} %get-tuple-element.14), custom_call_target="InvertDiagBlocksLowerTriangular" | custom-call | tf_op jit(solution)/shard_map/triangular_solve | solution.py:55
  (117 shorter events, 44.0 us)
Async XLA Ops:
  6.5 195.7 %all-gather.3.cloned.1.call-start = ((), (), s32[]{:S(2)}) async-start(), calls=%async_computation | async-start | bytes 8650752 | tf_op jit(solution)/shard_map/all_gather | solution.py:8
  9.5 9.4 %collective-permute-start = (bf16[1,1,64,2,256]{4,2,3,1,0:T(8,128)(2,1)S(1)}, bf16[1,1,64,2,256]{4,2,3,1,0:T(8,128)(2,1)S(1)}, u32[]{:S(2)}, u32[]{:S(2)}) collective-permute-start(bf16[1,1,64,2,256]{4,2,3,1,0:T(8,128)(2,1)S(1)} %select_bitcast_fusion.3), channel_id=1, source_target_pairs={{0,8},{8,16},{16,24},{1,9},{9,17},{17,25},{2,10},{10,18},{18,26},{... | collective-permute-start | bytes 196616 | tf_op jit(solution)/shard_map/ppermute | solution.py:17
  14.3 6.2 %collective-permute-start.1 = (bf16[1,1,64,2,256]{4,2,3,1,0:T(8,128)(2,1)S(1)}, bf16[1,1,64,2,256]{4,2,3,1,0:T(8,128)(2,1)S(1)}, u32[]{:S(2)}, u32[]{:S(2)}) collective-permute-start(bf16[1,1,64,2,256]{4,2,3,1,0:T(8,128)(2,1)S(1)} %select_bitcast_fusion.3), channel_id=1, source_target_pairs={{8,0},{16,8},{24,16},{9,1},{17,9},{25,17},{10,2},{18,10},{26,18},{... | collective-permute-start | bytes 196616 | tf_op jit(solution)/shard_map/ppermute | solution.py:20
  20.5 2.6 collective-permute-start.2
  21.8 5.1 %collective-permute-start.3 = (bf16[3,1,64,2,256]{4,2,3,1,0:T(8,128)(2,1)S(1)}, bf16[3,1,64,2,256]{4,2,3,1,0:T(8,128)(2,1)S(1)}, u32[]{:S(2)}, u32[]{:S(2)}) collective-permute-start(bf16[3,1,64,2,256]{4,2,3,1,0:T(8,128)(2,1)S(1)} %pad_maximum_fusion.1), channel_id=1, source_target_pairs={{1,0},{2,1},{3,2},{4,3},{5,4},{6,5},{7,6},{9,8},{10,9},{11,10},{12... | collective-permute-start | bytes 589832 | tf_op jit(solution)/shard_map/ppermute | solution.py:20
  28.1 7.3 %copy-start.5 = (bf16[64,2048]{1,0:T(8,128)(2,1)S(1)}, bf16[64,2048]{1,0:T(8,128)(2,1)}, u32[]{:S(2)}) copy-start(bf16[64,2048]{1,0:T(8,128)(2,1)} %param.9) | copy-start | bytes 786436
  36.7 6.2 %collective-permute-start.4 = (bf16[1,1,64,2,256]{4,2,3,1,0:T(8,128)(2,1)S(1)}, bf16[1,1,64,2,256]{4,2,3,1,0:T(8,128)(2,1)S(1)}, u32[]{:S(2)}, u32[]{:S(2)}) collective-permute-start(bf16[1,1,64,2,256]{4,2,3,1,0:T(8,128)(2,1)S(1)} %select_bitcast_fusion.2), channel_id=1, source_target_pairs={{0,8},{8,16},{16,24},{1,9},{9,17},{17,25},{2,10},{10,18},{18,26},{... | collective-permute-start | bytes 196616 | tf_op jit(solution)/shard_map/ppermute | solution.py:17
  41.0 6.6 %collective-permute-start.5 = (bf16[1,1,64,2,256]{4,2,3,1,0:T(8,128)(2,1)S(1)}, bf16[1,1,64,2,256]{4,2,3,1,0:T(8,128)(2,1)S(1)}, u32[]{:S(2)}, u32[]{:S(2)}) collective-permute-start(bf16[1,1,64,2,256]{4,2,3,1,0:T(8,128)(2,1)S(1)} %select_bitcast_fusion.2), channel_id=1, source_target_pairs={{8,0},{16,8},{24,16},{9,1},{17,9},{25,17},{10,2},{18,10},{26,18},{... | collective-permute-start | bytes 196616 | tf_op jit(solution)/shard_map/ppermute | solution.py:20
  47.6 5.6 %collective-permute-start.6 = (bf16[3,1,64,2,256]{4,2,3,1,0:T(8,128)(2,1)S(1)}, bf16[3,1,64,2,256]{4,2,3,1,0:T(8,128)(2,1)S(1)}, u32[]{:S(2)}, u32[]{:S(2)}) collective-permute-start(bf16[3,1,64,2,256]{4,2,3,1,0:T(8,128)(2,1)S(1)} %pad_maximum_fusion.2), channel_id=1, source_target_pairs={{0,1},{1,2},{2,3},{3,4},{4,5},{5,6},{6,7},{8,9},{9,10},{10,11},{11... | collective-permute-start | bytes 589832 | tf_op jit(solution)/shard_map/ppermute | solution.py:17
  51.8 4.2 %collective-permute-start.7 = (bf16[3,1,64,2,256]{4,2,3,1,0:T(8,128)(2,1)S(1)}, bf16[3,1,64,2,256]{4,2,3,1,0:T(8,128)(2,1)S(1)}, u32[]{:S(2)}, u32[]{:S(2)}) collective-permute-start(bf16[3,1,64,2,256]{4,2,3,1,0:T(8,128)(2,1)S(1)} %pad_maximum_fusion.2), channel_id=1, source_target_pairs={{1,0},{2,1},{3,2},{4,3},{5,4},{6,5},{7,6},{9,8},{10,9},{11,10},{12... | collective-permute-start | bytes 589832 | tf_op jit(solution)/shard_map/ppermute | solution.py:20
  65.1 19.6 %copy-start = (bf16[64,2048]{1,0:T(8,128)(2,1)}, bf16[64,2048]{1,0:T(8,128)(2,1)S(1)}, u32[]{:S(2)}) copy-start(bf16[64,2048]{1,0:T(8,128)(2,1)S(1)} %subtract_convert_fusion.2) | copy-start | bytes 786436
  65.8 5.7 %collective-permute-start.8 = (bf16[1,1,64,2,256]{4,2,3,1,0:T(8,128)(2,1)S(1)}, bf16[1,1,64,2,256]{4,2,3,1,0:T(8,128)(2,1)S(1)}, u32[]{:S(2)}, u32[]{:S(2)}) collective-permute-start(bf16[1,1,64,2,256]{4,2,3,1,0:T(8,128)(2,1)S(1)} %select_bitcast_fusion.1), channel_id=1, source_target_pairs={{0,8},{8,16},{16,24},{1,9},{9,17},{17,25},{2,10},{10,18},{18,26},{... | collective-permute-start | bytes 196616 | tf_op jit(solution)/shard_map/ppermute | solution.py:17
  69.6 6.4 %collective-permute-start.9 = (bf16[1,1,64,2,256]{4,2,3,1,0:T(8,128)(2,1)S(1)}, bf16[1,1,64,2,256]{4,2,3,1,0:T(8,128)(2,1)S(1)}, u32[]{:S(2)}, u32[]{:S(2)}) collective-permute-start(bf16[1,1,64,2,256]{4,2,3,1,0:T(8,128)(2,1)S(1)} %select_bitcast_fusion.1), channel_id=1, source_target_pairs={{8,0},{16,8},{24,16},{9,1},{17,9},{25,17},{10,2},{18,10},{26,18},{... | collective-permute-start | bytes 196616 | tf_op jit(solution)/shard_map/ppermute | solution.py:20
  76.1 5.7 %collective-permute-start.10 = (bf16[3,1,64,2,256]{4,2,3,1,0:T(8,128)(2,1)S(1)}, bf16[3,1,64,2,256]{4,2,3,1,0:T(8,128)(2,1)S(1)}, u32[]{:S(2)}, u32[]{:S(2)}) collective-permute-start(bf16[3,1,64,2,256]{4,2,3,1,0:T(8,128)(2,1)S(1)} %pad_maximum_fusion.3), channel_id=1, source_target_pairs={{0,1},{1,2},{2,3},{3,4},{4,5},{5,6},{6,7},{8,9},{9,10},{10,11},{11... | collective-permute-start | bytes 589832 | tf_op jit(solution)/shard_map/ppermute | solution.py:17
  80.5 4.2 %collective-permute-start.11 = (bf16[3,1,64,2,256]{4,2,3,1,0:T(8,128)(2,1)S(1)}, bf16[3,1,64,2,256]{4,2,3,1,0:T(8,128)(2,1)S(1)}, u32[]{:S(2)}, u32[]{:S(2)}) collective-permute-start(bf16[3,1,64,2,256]{4,2,3,1,0:T(8,128)(2,1)S(1)} %pad_maximum_fusion.3), channel_id=1, source_target_pairs={{1,0},{2,1},{3,2},{4,3},{5,4},{6,5},{7,6},{9,8},{10,9},{11,10},{12... | collective-permute-start | bytes 589832 | tf_op jit(solution)/shard_map/ppermute | solution.py:20
  85.8 7.3 %copy-start.1 = (bf16[64,2048]{1,0:T(8,128)(2,1)S(1)}, bf16[64,2048]{1,0:T(8,128)(2,1)}, u32[]{:S(2)}) copy-start(bf16[64,2048]{1,0:T(8,128)(2,1)} %copy-done) | copy-start | bytes 786436
  93.9 18.4 %copy-start.3 = (bf16[64,2048]{1,0:T(8,128)(2,1)}, bf16[64,2048]{1,0:T(8,128)(2,1)S(1)}, u32[]{:S(2)}) copy-start(bf16[64,2048]{1,0:T(8,128)(2,1)S(1)} %subtract_convert_fusion.1) | copy-start | bytes 786436
  94.6 4.6 %collective-permute-start.12 = (bf16[1,1,64,2,256]{4,2,3,1,0:T(8,128)(2,1)S(1)}, bf16[1,1,64,2,256]{4,2,3,1,0:T(8,128)(2,1)S(1)}, u32[]{:S(2)}, u32[]{:S(2)}) collective-permute-start(bf16[1,1,64,2,256]{4,2,3,1,0:T(8,128)(2,1)S(1)} %select_bitcast_fusion), channel_id=1, source_target_pairs={{0,8},{8,16},{16,24},{1,9},{9,17},{17,25},{2,10},{10,18},{18,26},{... | collective-permute-start | bytes 196616 | tf_op jit(solution)/shard_map/ppermute | solution.py:17
  97.3 6.4 %collective-permute-start.13 = (bf16[1,1,64,2,256]{4,2,3,1,0:T(8,128)(2,1)S(1)}, bf16[1,1,64,2,256]{4,2,3,1,0:T(8,128)(2,1)S(1)}, u32[]{:S(2)}, u32[]{:S(2)}) collective-permute-start(bf16[1,1,64,2,256]{4,2,3,1,0:T(8,128)(2,1)S(1)} %select_bitcast_fusion), channel_id=1, source_target_pairs={{8,0},{16,8},{24,16},{9,1},{17,9},{25,17},{10,2},{18,10},{26,18},{... | collective-permute-start | bytes 196616 | tf_op jit(solution)/shard_map/ppermute | solution.py:20
  103.7 5.9 %collective-permute-start.14 = (bf16[3,1,64,2,256]{4,2,3,1,0:T(8,128)(2,1)S(1)}, bf16[3,1,64,2,256]{4,2,3,1,0:T(8,128)(2,1)S(1)}, u32[]{:S(2)}, u32[]{:S(2)}) collective-permute-start(bf16[3,1,64,2,256]{4,2,3,1,0:T(8,128)(2,1)S(1)} %pad_maximum_fusion.4), channel_id=1, source_target_pairs={{0,1},{1,2},{2,3},{3,4},{4,5},{5,6},{6,7},{8,9},{9,10},{10,11},{11... | collective-permute-start | bytes 589832 | tf_op jit(solution)/shard_map/ppermute | solution.py:17
  108.1 4.2 %collective-permute-start.15 = (bf16[3,1,64,2,256]{4,2,3,1,0:T(8,128)(2,1)S(1)}, bf16[3,1,64,2,256]{4,2,3,1,0:T(8,128)(2,1)S(1)}, u32[]{:S(2)}, u32[]{:S(2)}) collective-permute-start(bf16[3,1,64,2,256]{4,2,3,1,0:T(8,128)(2,1)S(1)} %pad_maximum_fusion.4), channel_id=1, source_target_pairs={{1,0},{2,1},{3,2},{4,3},{5,4},{6,5},{7,6},{9,8},{10,9},{11,10},{12... | collective-permute-start | bytes 589832 | tf_op jit(solution)/shard_map/ppermute | solution.py:20
  113.4 7.4 %copy-start.4 = (bf16[64,2048]{1,0:T(8,128)(2,1)S(1)}, bf16[64,2048]{1,0:T(8,128)(2,1)}, u32[]{:S(2)}) copy-start(bf16[64,2048]{1,0:T(8,128)(2,1)} %copy-done.3) | copy-start | bytes 786436
  113.4 8.1 %copy-start.2 = (bf16[64,2048]{1,0:T(8,128)(2,1)S(1)}, bf16[64,2048]{1,0:T(8,128)(2,1)}, u32[]{:S(2)}) copy-start(bf16[64,2048]{1,0:T(8,128)(2,1)} %copy-done) | copy-start | bytes 786436
Sparse Core Ops, SparseCore 0:
  122.8 79.3 all-gather.2
